TPU v7x, 32 devices: a whole 2x2x4 slice. The times are simulated.
32 devices in a mesh: ctx: 8 (over y, x, core), dp: 4 (over z).
Axes of the slice: x: 2, y: 2, z: 4, core: 2. Of those that a mesh axis runs over, the one named last changes fastest.
Arguments:
- ids: int32 [3072], P('ctx'), may hold values from 0 to 511
- embed_table: bfloat16 [512, 4096], P(None, 'dp'), may hold values from -6 to 6
- norm_gain: bfloat16 [4096], P('dp'), may hold values from 0.25 to 1.75
- w_query: bfloat16 [4096, 4096], P('ctx', 'dp'), may hold values from -0.09375 to 0.09375
- w_key: bfloat16 [4096, 4096], P('ctx', 'dp'), may hold values from -0.09375 to 0.09375
- w_value: bfloat16 [4096, 4096], P('ctx', 'dp'), may hold values from -0.09375 to 0.09375
- short_filter: float32 [3, 3, 4096], P(None, None, 'dp'), may hold values from -4 to 4
- pole_rate: float32 [4096, 16], P('dp'), may hold values from 1.6276042e-05 to 0.05
- residue: float32 [4096, 16], P('dp'), may hold values from -2 to 2
- skip_gain: float32 [4096], P('dp'), may hold values from -4 to 4
- w_out: bfloat16 [4096, 4096], P('ctx', 'dp'), may hold values from -0.09375 to 0.09375
Outputs:
- block_out: bfloat16 [3072, 4096], P('ctx', 'dp')
All inputs are finite; a program needn't handle non-finite values.
Results may differ from a plain program's by a relative error of at most 0.0082.
Values may be sent and summed in bfloat16 or wider, within the bound.
A program may use at most 128 MiB of HBM per device.

v0:
```python
import math
import jax
import jax.numpy as jnp
from jax import lax
from jax.sharding import PartitionSpec as P


def shifted(value, axis, steps):
    count = lax.axis_size(axis)
    initial, last = (max(0, -steps), min(count, count - steps))
    return lax.ppermute(value, axis, [(source, source + steps) for source in range(initial, last)])


def entering_2(value, axis, combine, identity):
    peers, index = (lax.axis_size(axis), lax.axis_index(axis))
    everything = jax.tree.map(lambda part: lax.all_gather(part, axis), value)
    start = jax.tree.map(
        lambda part, zero: jnp.broadcast_to(jnp.asarray(zero, part.dtype), part.shape),
        value,
        identity,
    )

    def turn(k, before):
        reached = k < index
        new = combine(before, jax.tree.map(lambda part: part[k], everything))
        return jax.tree.map(lambda a, b: jnp.where(reached, a, b), new, before)

    return lax.fori_loop(0, peers, turn, start)


def shards(
    ids,
    embed_table,
    norm_gain,
    w_query,
    w_key,
    w_value,
    short_filter,
    pole_rate,
    residue,
    skip_gain,
    w_out,
):
    highest = lax.Precision.HIGHEST
    vocab = embed_table.shape[0]
    channels = w_query.shape[1]
    one_hot = (ids[:, None] == jnp.arange(vocab, dtype=jnp.int32)[None, :]).astype(jnp.bfloat16)
    embedded = jnp.dot(one_hot, embed_table, preferred_element_type=jnp.float32).astype(
        jnp.bfloat16
    )
    full_rows, full_gain = (
        lax.all_gather(embedded, "dp", axis=1, tiled=True),
        lax.all_gather(norm_gain, "dp", axis=0, tiled=True),
    )
    floated = full_rows.astype(jnp.float32)
    scale = lax.rsqrt(jnp.mean(floated * floated, axis=1, keepdims=True) + 1e-06)
    normed = (floated * scale * full_gain.astype(jnp.float32)[None, :]).astype(jnp.bfloat16)
    tok_rows = normed.shape[0]

    def add_rows(piece):
        return jnp.dot(normed, piece, preferred_element_type=jnp.float32)

    query_proj = add_rows(lax.all_gather(w_query, "ctx", axis=0, tiled=True))
    key_proj = add_rows(lax.all_gather(w_key, "ctx", axis=0, tiled=True))
    value_proj = add_rows(lax.all_gather(w_value, "ctx", axis=0, tiled=True))
    projected = jnp.concatenate([query_proj, key_proj, value_proj], axis=1).astype(jnp.bfloat16)
    taps = short_filter.shape[0]
    previous = shifted(projected[tok_rows - (taps - 1) :], "ctx", 1)
    extended = jnp.concatenate([previous, projected], axis=0).astype(jnp.float32)
    filt_rows = short_filter.reshape(taps, 3 * channels)
    convolved = jnp.zeros((tok_rows, 3 * channels), jnp.float32)
    for tap in range(taps):
        convolved = (
            convolved
            + filt_rows[tap][None, :] * extended[taps - 1 - tap : taps - 1 - tap + tok_rows]
        )
    query_conv = convolved[:, :channels]
    gated = convolved[:, channels : 2 * channels] * convolved[:, 2 * channels :]
    sub_len = math.gcd(tok_rows, 64)
    blocks = tok_rows // sub_len
    lag_index = jnp.arange(sub_len, dtype=jnp.int32)
    lags = lag_index.astype(jnp.float32)
    strength = residue * jnp.sqrt(2.0 * pole_rate)
    kernel = jnp.einsum(
        "lck,ck->lc", jnp.exp(-pole_rate[None] * lags[:, None, None]), strength, precision=highest
    )
    offsets = lag_index[:, None] - lag_index[None, :]
    toeplitz = jnp.where((offsets >= 0)[:, :, None], kernel[jnp.maximum(offsets, 0)], 0.0)
    pieces = gated.reshape(blocks, sub_len, channels)
    inside = jnp.einsum("tsc,bsc->btc", toeplitz, pieces, precision=highest)
    tail_decay = jnp.exp(-pole_rate[None] * (sub_len - 1.0 - lags)[:, None, None])
    block_ends = jnp.einsum("sck,bsc->bck", tail_decay, pieces, precision=highest)
    step_decay = jnp.exp(-pole_rate * float(sub_len))

    def advance(state, block_end):
        return (step_decay * state + block_end, state)

    device_end, entering = lax.scan(advance, jnp.zeros_like(step_decay), block_ends)
    device_decay = jnp.exp(-pole_rate * float(tok_rows))

    def combine(earlier, later):
        return (earlier[0] * later[0], later[0] * earlier[1] + later[1])

    decay_total, incoming = entering_2(
        (device_decay, device_end),
        "ctx",
        combine,
        (jnp.ones_like(device_decay), jnp.zeros_like(device_end)),
    )
    block_pos = jnp.arange(blocks, dtype=jnp.float32) * float(sub_len)
    states_in = entering + jnp.exp(-pole_rate[None] * block_pos[:, None, None]) * incoming[None]
    lead = jnp.exp(-pole_rate[None] * (lags + 1.0)[:, None, None]) * strength[None]
    carried = jnp.einsum("tck,bck->btc", lead, states_in, precision=highest)
    long_conv = (inside + carried).reshape(tok_rows, channels) + skip_gain[None, :] * gated
    mixed = (query_conv * long_conv).astype(jnp.bfloat16)
    all_mixed = lax.all_gather(mixed, "dp", axis=1, tiled=True)
    output = jnp.dot(
        all_mixed,
        lax.all_gather(w_out, "ctx", axis=0, tiled=True),
        preferred_element_type=jnp.float32,
    )
    return (embedded.astype(jnp.float32) + output).astype(jnp.bfloat16)


def solution(mesh):
    placed = (
        P("ctx"),
        P(None, "dp"),
        P("dp"),
        P("ctx", "dp"),
        P("ctx", "dp"),
        P("ctx", "dp"),
        P(None, None, "dp"),
        P("dp", None),
        P("dp", None),
        P("dp"),
        P("ctx", "dp"),
    )
    return jax.shard_map(
        shards, mesh=mesh, in_specs=placed, out_specs=P("ctx", "dp"), check_vma=False
    )
```

profile of v0, /device:TPU:0, one launch (start us, length us, event | category | flops | bytes accessed | tf_op | source)
XLA Modules:
  0.0 511.5 jit_solution(16965274444478616923)
XLA Ops:
  6.6 1.2 copy-done
  7.8 2.2 convolution_convert_fusion.3
  10.0 0.7 all-gather.15.cloned.1.call-update
  10.8 0.7 all-gather.13.cloned.1.call-update
  11.5 0.5 all-gather.11.cloned.1.call-update
  12.1 0.5 all-gather.19.cloned.1.call-update
  13.3 12.5 %multiply_reduce_fusion = f32[1024,64]{1,0:T(8,128)} fusion(f32[1024,16]{1,0:T(8,128)S(1)} %copy.47, f32[64]{0:T(128)S(1)} %iota_convert_fusion, f32[1024,16]{1,0:T(8,128)S(1)} %copy.30), kind=kLoop, calls=%fused_computation.14 | loop fusion | flops 3080192 | bytes 393472
  25.9 14.8 %all_gather.34 = bf16[4096]{0:T(1024)(128)(2,1)S(1)} all-gather(bf16[1024]{0:T(1024)(128)(2,1)S(1)} %copy-done.12), channel_id=1, replica_groups=mesh['ctx'=8,'dp'=4] {'dp'}, dimensions={0}, use_global_device_ids=true | all-gather | bytes 10240 | tf_op jit(solution)/shard_map/all_gather | solution.py:53
  40.7 10.9 %all-gather = f32[8192,16]{0,1:T(8,128)} all-gather(f32[1024,16]{0,1:T(8,128)S(1)} %get-tuple-element.213), channel_id=2, replica_groups=mesh['ctx'=8,'dp'=4] {'ctx'}, dimensions={0}, use_global_device_ids=true | all-gather | bytes 589824 | tf_op jit(solution)/shard_map/all_gather | solution.py:16
  51.6 24.7 %all-gather.9.cloned.1.call-done = bf16[384,4096]{1,0:T(8,128)(2,1)} async-done(((bf16[384,1024]{1,0:T(8,128)(2,1)}), bf16[384,4096]{1,0:T(8,128)(2,1)}) %all-gather.9.cloned.1.call-update) | async-done | bytes 3145744 | tf_op jit(solution)/shard_map/all_gather | solution.py:52
  76.3 2.6 fusion.14
  78.9 52.2 %all-gather.15.cloned.1.call-done = bf16[4096,1024]{1,0:T(8,128)(2,1)} async-done(((bf16[512,1024]{1,0:T(8,128)(2,1)}), bf16[4096,1024]{1,0:T(8,128)(2,1)}) %all-gather.15.cloned.1.call-update) | async-done | bytes 8388624 | tf_op jit(solution)/shard_map/all_gather | solution.py:65
  131.2 7.8 %convolution_convert_fusion = bf16[384,1024]{1,0:T(8,128)(2,1)S(1)} fusion(bf16[4096,1024]{1,0:T(8,128)(2,1)} %all-gather.15.cloned.1.call-done, bf16[384,4096]{1,0:T(8,128)(2,1)} %all-gather.9.cloned.1.call-done, f32[4096]{0:T(1024)S(1)} %convert_element_type.46, f32[384]{0:T(512)S(1)} %add_rsqrt_fusion), kind=kOutput, calls=%fused_computation.45 | convolution fusion | flops 3227910144 | bytes 12338688 | tf_op jit(solution)/shard_map/dot_general | solution.py:61
  139.0 48.4 %all-gather.13.cloned.1.call-done = bf16[4096,1024]{1,0:T(8,128)(2,1)} async-done(((bf16[512,1024]{1,0:T(8,128)(2,1)}), bf16[4096,1024]{1,0:T(8,128)(2,1)}) %all-gather.13.cloned.1.call-update) | async-done | bytes 8388624 | tf_op jit(solution)/shard_map/all_gather | solution.py:64
  187.3 7.8 %convolution_convert_fusion.1 = bf16[384,1024]{1,0:T(8,128)(2,1)S(1)} fusion(bf16[4096,1024]{1,0:T(8,128)(2,1)} %all-gather.13.cloned.1.call-done, bf16[384,4096]{1,0:T(8,128)(2,1)} %all-gather.9.cloned.1.call-done, f32[4096]{0:T(1024)S(1)} %convert_element_type.46, f32[384]{0:T(512)S(1)} %add_rsqrt_fusion), kind=kOutput, calls=%fused_computation.46 | convolution fusion | flops 3227910144 | bytes 12338688 | tf_op jit(solution)/shard_map/dot_general | solution.py:61
  195.1 48.2 %all-gather.11.cloned.1.call-done = bf16[4096,1024]{1,0:T(8,128)(2,1)} async-done(((bf16[512,1024]{1,0:T(8,128)(2,1)}), bf16[4096,1024]{1,0:T(8,128)(2,1)}) %all-gather.11.cloned.1.call-update) | async-done | bytes 8388624 | tf_op jit(solution)/shard_map/all_gather | solution.py:63
  243.4 7.8 %convolution_convert_fusion.2 = bf16[384,1024]{1,0:T(8,128)(2,1)S(1)} fusion(bf16[4096,1024]{1,0:T(8,128)(2,1)} %all-gather.11.cloned.1.call-done, bf16[384,4096]{1,0:T(8,128)(2,1)} %all-gather.9.cloned.1.call-done, f32[4096]{0:T(1024)S(1)} %convert_element_type.46, f32[384]{0:T(512)S(1)} %add_rsqrt_fusion), kind=kOutput, calls=%fused_computation.47 | convolution fusion | flops 3227910144 | bytes 12338688 | tf_op jit(solution)/shard_map/dot_general | solution.py:61
  251.2 2.2 collective-permute-start
  253.5 1.2 copy.44
  254.7 18.9 %gather_fusion = f32[4096,1024]{1,0:T(8,128)} fusion(f32[64,1024]{1,0:T(8,128)S(1)} %bitcast.57, s32[4096]{0:T(1024)S(1)} %broadcast_clamp_fusion), kind=kCustom, calls=%fused_computation | custom fusion | bytes 33570816 | tf_op jit(solution)/shard_map/gather | solution.py:88
  273.6 30.7 %copy.31 = f32[64,64,1024]{1,0,2:T(8,128)} copy(f32[64,64,1024]{2,1,0:T(8,128)} %bitcast.58) | data formatting | bytes 33554432 | tf_op jit(solution)/shard_map/gather | solution.py:88
  304.3 2.1 copy.48
  306.5 0.7 maximum_convert_fusion
  307.2 1.4 fusion.17
  308.6 2.2 copy-done.2
  310.8 0.3 slice_multiply_fusion.3
  311.1 2.7 copy.32
  313.8 16.9 %fusion.24 = f32[6,1024,16]{2,0,1:T(8,128)} fusion(f32[6,64,1024]{1,0,2:T(8,128)} %copy.32, f32[64]{0:T(128)S(1)} %broadcast_subtract_fusion, f32[1024,16]{1,0:T(8,128)S(1)} %copy.30), kind=kOutput, calls=%fused_computation.39 | convolution fusion | flops 76546048 | bytes 2031872 | tf_op jit(solution)/shard_map/sck,bsc->bck/dot_general | solution.py:92
  330.7 2.7 copy.34
  333.4 0.4 while.27
  333.8 10.3 %all-gather.1 = f32[8192,16]{0,1:T(8,128)S(1)} all-gather(f32[1024,16]{0,1:T(8,128)S(1)} %get-tuple-element.128), channel_id=3, replica_groups=mesh['ctx'=8,'dp'=4] {'ctx'}, dimensions={0}, use_global_device_ids=true | all-gather | bytes 589824 | tf_op jit(solution)/shard_map/all_gather | solution.py:16
  344.0 0.3 copy.49
  344.3 9.8 %while.28 = (s32[]{:T(128)}, f32[1024,16]{0,1:T(8,128)S(1)}, s32[]{:T(128)}, f32[8,1024,16]{1,0,2:T(8,128)}, f32[8,1024,16]{1,0,2:T(8,128)S(1)}, /*index=5*/s32[]{:T(128)}, s32[]{:T(128)}) while((s32[]{:T(128)}, f32[1024,16]{0,1:T(8,128)S(1)}, s32[]{:T(128)}, f32[8,1024,16]{1,0,2:T(8,128)}, f32[8,1024,16]{1,0,2:T(8,128)S(1)}, ...), condition=%wide.region_4.5_spmd.clone, body=%wide.region_3.4_spmd.clone.sunk | while | flops 65540 | bytes 524397 | solution.py:28
  344.3 1.1 constant_dynamic-slice_fusion.3
  345.6 1.1 constant_dynamic-slice_fusion.3
  346.8 1.1 constant_dynamic-slice_fusion.3
  348.0 1.1 constant_dynamic-slice_fusion.3
  349.2 1.1 constant_dynamic-slice_fusion.3
  350.4 1.1 constant_dynamic-slice_fusion.3
  351.7 1.1 constant_dynamic-slice_fusion.3
  352.9 1.1 constant_dynamic-slice_fusion.3
  354.2 2.7 copy.38
  356.9 56.2 %fusion.3 = f32[1024,6,64]{2,1,0:T(8,128)S(1)} fusion(f32[6,64,1024]{1,0,2:T(8,128)} %copy.32, f32[64,64,1024]{1,0,2:T(8,128)} %copy.31, pred[64,64]{1,0:T(8,128)(4,1)S(1)} %subtract_compare_fusion), kind=kOutput, calls=%fused_computation.10 | convolution fusion | flops 306184192 | bytes 19927040 | tf_op jit(solution)/shard_map/tsc,bsc->btc/dot_general | solution.py:90
  413.2 12.3 %add_bitcast_fusion = f32[6,64,1024]{1,0,2:T(8,128)} fusion(f32[1024,6,64]{2,1,0:T(8,128)S(1)} %fusion.3, f32[6,1024,16]{2,0,1:T(8,128)S(1)} %copy-done.3, f32[1024,16]{1,0:T(8,128)S(1)} %copy-done.6, f32[64]{0:T(128)S(1)} %broadcast_add_fusion, f32[1024,16]{1,0:T(8,128)S(1)} %copy.30), kind=kOutput, calls=%fused_computation.32 | convolution fusion | flops 77987840 | bytes 3670272 | tf_op jit(solution)/shard_map/tck,bck->btc/dot_general | solution.py:113
  425.5 2.7 copy.39
  428.2 3.9 fusion.29
  432.2 63.5 %all-gather.17.cloned.1.call-done = bf16[384,4096]{1,0:T(8,128)(2,1)} async-done(((bf16[384,1024]{1,0:T(8,128)(2,1)}), bf16[384,4096]{1,0:T(8,128)(2,1)}) %all-gather.17.cloned.1.call-update) | async-done | bytes 3145744 | tf_op jit(solution)/shard_map/all_gather | solution.py:116
  495.8 8.7 %add_convert_fusion = bf16[384,1024]{1,0:T(8,128)(2,1)} fusion(bf16[384,1024]{1,0:T(8,128)(2,1)S(1)} %copy-done.4, bf16[384,4096]{1,0:T(8,128)(2,1)} %all-gather.17.cloned.1.call-done, bf16[4096,1024]{1,0:T(8,128)(2,1)} %all-gather.19.cloned.1.call-done), kind=kOutput, calls=%fused_computation.44 | convolution fusion | flops 3222405120 | bytes 13107200 | tf_op jit(solution)/shard_map/dot_general | solution.py:117
  (76 shorter events, 1.7 us)
Async XLA Ops:
  6.5 1.2 copy-start
  6.5 6.2 %copy-start.10 = (f32[3,3,1024]{2,1,0:T(4,128)S(1)}, f32[3,3,1024]{2,1,0:T(4,128)}, u32[]{:S(2)}) copy-start(f32[3,3,1024]{2,1,0:T(4,128)} %param.21) | copy-start | bytes 110596
  6.5 6.2 %copy-start.8 = (f32[1024,16]{0,1:T(8,128)S(1)}, f32[1024,16]{0,1:T(8,128)}, u32[]{:S(2)}) copy-start(f32[1024,16]{0,1:T(8,128)} %param.22) | copy-start | bytes 196612
  6.5 6.2 %copy-start.9 = (f32[1024,16]{0,1:T(8,128)S(1)}, f32[1024,16]{0,1:T(8,128)}, u32[]{:S(2)}) copy-start(f32[1024,16]{0,1:T(8,128)} %param.23) | copy-start | bytes 196612
  6.5 69.8 %all-gather.9.cloned.1.call-start = ((), (), s32[]{:S(2)}) async-start(), calls=%async_computation | async-start | bytes 3932160 | tf_op jit(solution)/shard_map/all_gather | solution.py:52
  9.9 15.9 %copy-start.12 = (bf16[1024]{0:T(1024)(128)(2,1)S(1)}, bf16[1024]{0:T(1024)(128)(2,1)}, u32[]{:S(2)}) copy-start(bf16[1024]{0:T(1024)(128)(2,1)} %param.17) | copy-start | bytes 6148
  10.0 121.2 %all-gather.15.cloned.1.call-start = ((), (), s32[]{:S(2)}) async-start(), calls=%async_computation.3 | async-start | bytes 9437184 | tf_op jit(solution)/shard_map/all_gather | solution.py:65
  10.7 176.6 %all-gather.13.cloned.1.call-start = ((), (), s32[]{:S(2)}) async-start(), calls=%async_computation.2 | async-start | bytes 9437184 | tf_op jit(solution)/shard_map/all_gather | solution.py:64
  11.5 231.9 %all-gather.11.cloned.1.call-start = ((), (), s32[]{:S(2)}) async-start(), calls=%async_computation.1 | async-start | bytes 9437184 | tf_op jit(solution)/shard_map/all_gather | solution.py:63
  12.0 420.2 %all-gather.19.cloned.1.call-start = ((), (), s32[]{:S(2)}) async-start(), calls=%async_computation.5 | async-start | bytes 9437184 | tf_op jit(solution)/shard_map/all_gather | solution.py:119
  12.6 483.1 %all-gather.17.cloned.1.call-start = ((), (), s32[]{:S(2)}) async-start(), calls=%async_computation.4 | async-start | bytes 3932160 | tf_op jit(solution)/shard_map/all_gather | solution.py:116
  13.0 65.9 %copy-start.5 = (f32[1024,16]{1,0:T(8,128)}, f32[1024,16]{1,0:T(8,128)S(1)}, u32[]{:S(2)}) copy-start(f32[1024,16]{1,0:T(8,128)S(1)} %copy.47) | copy-start | bytes 196612
  251.2 55.3 %collective-permute-start = (bf16[2,3072]{1,0:T(2,128)(2,1)S(1)}, bf16[2,3072]{1,0:T(2,128)(2,1)S(1)}, u32[]{:S(2)}, u32[]{:S(2)}) collective-permute-start(bf16[2,3072]{1,0:T(2,128)(2,1)S(1)} %pad_maximum_fusion), channel_id=1, source_target_pairs={{0,4},{4,8},{8,12},{12,16},{16,20},{20,24},{24,28},{1,5},{5,9},{9,... | collective-permute-start | bytes 36872 | tf_op jit(solution)/shard_map/ppermute | solution.py:11
  308.6 2.2 copy-start.2
  313.8 19.5 %copy-start.7 = (f32[6,1024,16]{1,2,0:T(8,128)S(1)}, f32[6,1024,16]{1,2,0:T(8,128)}, u32[]{:S(2)}) copy-start(f32[6,1024,16]{1,2,0:T(8,128)} %custom-call.4) | copy-start | bytes 1179652
  356.9 56.2 %copy-start.3 = (f32[6,1024,16]{2,0,1:T(8,128)S(1)}, f32[6,1024,16]{2,0,1:T(8,128)}, u32[]{:S(2)}) copy-start(f32[6,1024,16]{2,0,1:T(8,128)} %copy.38) | copy-start | bytes 1179652
  356.9 56.2 %copy-start.6 = (f32[1024,16]{1,0:T(8,128)S(1)}, f32[1024,16]{1,0:T(8,128)}, u32[]{:S(2)}) copy-start(f32[1024,16]{1,0:T(8,128)} %copy-done.5) | copy-start | bytes 196612
  425.5 2.7 copy-start.11
  428.2 67.5 %copy-start.4 = (bf16[384,1024]{1,0:T(8,128)(2,1)S(1)}, bf16[384,1024]{1,0:T(8,128)(2,1)}, u32[]{:S(2)}) copy-start(bf16[384,1024]{1,0:T(8,128)(2,1)} %convolution_convert_fusion.3) | copy-start | bytes 2359300
  495.8 8.7 %copy-start.1 = (bf16[512,1024]{1,0:T(8,128)(2,1)S(1)}, bf16[512,1024]{1,0:T(8,128)(2,1)}, u32[]{:S(2)}) copy-start(bf16[512,1024]{1,0:T(8,128)(2,1)} %param.16) | copy-start | bytes 3145732
Sparse Core Ops, SparseCore 0:
  10.1 66.2 all-gather.8
  78.2 52.8 all-gather.14
  133.0 54.2 all-gather.12
  189.1 54.2 all-gather.10
  245.1 54.2 all-gather.18
  432.3 63.4 all-gather.16
where the time goes:
time: 521 us; the launch traced here: 512 us
  waiting for transfers between devices  240 us (46%)
  matrix products  120 us (23%)
  local copies, waits for them, and re-layouts  77.3 us (15%)
  blocking collectives  36 us (7%)
  other arithmetic  22.2 us (4%)
  between operations  14 us (3%)
    all_gather x1, waiting for transfers between devices, shards(): all_mixed = lax.all_gather(mixed, 'dp', axis=1, tiled=True)  63.5 us
    dot_general x1, matrix products, shards(): inside = jnp.einsum('tsc,bsc->btc', toeplitz, pieces, precision=highest)  56.2 us
    all_gather x1, waiting for transfers between devices, shards(): value_proj = add_rows(lax.all_gather(w_value, 'ctx', axis=0, tiled=True))  52.2 us
    gather x2, local copies, waits for them, and re-layouts, shards(): kernel[jnp.maximum(offsets, 0)]  49.6 us
    all_gather x1, waiting for transfers between devices, shards(): key_proj = add_rows(lax.all_gather(w_key, 'ctx', axis=0, tiled=True))  48.4 us
    all_gather x1, waiting for transfers between devices, shards(): query_proj = add_rows(lax.all_gather(w_query, 'ctx', axis=0, tiled=True))  48.2 us
    all_gather x1, waiting for transfers between devices, shards(): lax.all_gather(embedded, 'dp', axis=1, tiled=True)  24.7 us
    dot_general x3, matrix products, add_rows(): return jnp.dot(normed, piece, preferred_element_type=jnp.float32)  23.4 us
  transfers between devices with their start and end apart: 7, of which 5 were waited for; matrix products, arithmetic and copies ran while one was open for 40% of the time, Pallas kernels for 0%

commit v1 on v0

--- a/solution.py
+++ b/solution.py
@@ -3,6 +3,12 @@
 import jax.numpy as jnp
 from jax import lax
 from jax.sharding import PartitionSpec as P
+
+
+def gather_by_exchange(x, axis, dim):
+    peers = lax.axis_size(axis)
+    repeats = [peers if d == dim else 1 for d in range(x.ndim)]
+    return lax.all_to_all(jnp.tile(x, repeats), axis, split_axis=dim, concat_axis=dim, tiled=True)
 
 
 def shifted(value, axis, steps):
@@ -60,7 +66,7 @@
     def add_rows(piece):
         return jnp.dot(normed, piece, preferred_element_type=jnp.float32)
 
-    query_proj = add_rows(lax.all_gather(w_query, "ctx", axis=0, tiled=True))
+    query_proj = add_rows(gather_by_exchange(w_query, "ctx", 0))
     key_proj = add_rows(lax.all_gather(w_key, "ctx", axis=0, tiled=True))
     value_proj = add_rows(lax.all_gather(w_value, "ctx", axis=0, tiled=True))
     projected = jnp.concatenate([query_proj, key_proj, value_proj], axis=1).astype(jnp.bfloat16)

time: 521 us -> 482 us (0.925)
  waiting for transfers between devices: 240 us -> 119 us
  blocking collectives: 36 us -> 113 us
  starting transfers between devices: 2.38 us -> 7.65 us
    all_gather x2, blocking collectives: 21.1 us -> 98.6 us  [entering_2(): everything = jax.tree.map(lambda part: lax.all_gather(part, axis), value)]
    all_gather x1 -> x0, waiting for transfers between devices: 48.2 us -> none  [shards(): query_proj = add_rows(lax.all_gather(w_query, 'ctx', axis=0, tiled=True))]
    all_gather x1, waiting for transfers between devices: 52.2 us -> 4.74 us  [shards(): value_proj = add_rows(lax.all_gather(w_value, 'ctx', axis=0, tiled=True))]
    all_gather x1, waiting for transfers between devices: 24.7 us -> 0.01 us  [shards(): lax.all_gather(embedded, 'dp', axis=1, tiled=True)]
    all_to_all x0 -> x1, starting transfers between devices: none -> 5.33 us  [gather_by_exchange(): lax.all_to_all(jnp.tile(x, repeats), axis, split_axis=dim, concat_axis=di...]
  transfers between devices with their start and end apart: 7 -> 7, of which waited for: 5 -> 3; matrix products, arithmetic and copies ran while one was open for 40% -> 44% of each run, Pallas kernels for 0% -> 0%
where the time goes in v1:
time: 482 us; the launch traced here: 477 us
  matrix products  120 us (25%)
  waiting for transfers between devices  119 us (25%)
  blocking collectives  113 us (23%)
  local copies, waits for them, and re-layouts  81.5 us (17%)
  other arithmetic  22.2 us (5%)
  between operations  13.7 us (3%)
  starting transfers between devices  7.65 us (2%)
    all_gather x2, blocking collectives, entering_2(): everything = jax.tree.map(lambda part: lax.all_gather(part, axis), value)  98.6 us
    all_gather x1, waiting for transfers between devices, shards(): all_mixed = lax.all_gather(mixed, 'dp', axis=1, tiled=True)  63.5 us
    dot_general x1, matrix products, shards(): inside = jnp.einsum('tsc,bsc->btc', toeplitz, pieces, precision=highest)  56.2 us
    gather x2, local copies, waits for them, and re-layouts, shards(): kernel[jnp.maximum(offsets, 0)]  49.5 us
    all_gather x1, waiting for transfers between devices, shards(): key_proj = add_rows(lax.all_gather(w_key, 'ctx', axis=0, tiled=True))  49.1 us
    dot_general x3, matrix products, add_rows(): return jnp.dot(normed, piece, preferred_element_type=jnp.float32)  23.4 us
    dot_general x1, matrix products, shards(): jnp.einsum('sck,bsc->bck', tail_decay, pieces, precision=highest)  16.9 us
    all_gather x1, blocking collectives, shards(): lax.all_gather(norm_gain, 'dp', axis=0, tiled=True)  14.2 us
  transfers between devices with their start and end apart: 7, of which 3 were waited for; matrix products, arithmetic and copies ran while one was open for 44% of the time, Pallas kernels for 0%

profile of v1, /device:TPU:0, one launch (start us, length us, event | category | flops | bytes accessed | tf_op | source)
XLA Modules:
  0.0 477.3 jit_solution(15558252561068745203)
XLA Ops:
  6.5 1.2 copy-done
  7.8 2.2 convolution_convert_fusion.3
  10.0 0.7 all-gather.12.cloned.1.call-update
  10.8 0.7 all-gather.10.cloned.1.call-update
  11.5 4.3 tile.2
  15.8 5.3 %all-to-all-start = ((bf16[8,512,1024]{2,1,0:T(8,128)(2,1)}), bf16[8,512,1024]{2,1,0:T(8,128)(2,1)}, u32[]{:S(2)}, u32[]{:S(2)}) async-start(bf16[8,512,1024]{2,1,0:T(8,128)(2,1)} %tile.2), calls=%async_computation | async-start | bytes 16777216 | tf_op jit(solution)/shard_map/all_to_all | solution.py:11
  21.2 0.5 all-gather.16.cloned.1.call-update
  21.8 0.2 copy.47
  22.4 12.6 %multiply_reduce_fusion = f32[1024,64]{1,0:T(8,128)} fusion(f32[1024,16]{1,0:T(8,128)S(1)} %copy.47, f32[64]{0:T(128)S(1)} %iota_convert_fusion, f32[1024,16]{1,0:T(8,128)S(1)} %copy.30), kind=kLoop, calls=%fused_computation.14 | loop fusion | flops 3080192 | bytes 393472
  35.0 14.2 %all_gather.31 = bf16[4096]{0:T(1024)(128)(2,1)S(1)} all-gather(bf16[1024]{0:T(1024)(128)(2,1)S(1)} %copy-done.13), channel_id=1, replica_groups=mesh['ctx'=8,'dp'=4] {'dp'}, dimensions={0}, use_global_device_ids=true | all-gather | bytes 10240 | tf_op jit(solution)/shard_map/all_gather | solution.py:59
  49.1 88.5 %all-gather = f32[8192,16]{0,1:T(8,128)} all-gather(f32[1024,16]{0,1:T(8,128)S(1)} %get-tuple-element.213), channel_id=2, replica_groups=mesh['ctx'=8,'dp'=4] {'ctx'}, dimensions={0}, use_global_device_ids=true | all-gather | bytes 589824 | tf_op jit(solution)/shard_map/all_gather | solution.py:22
  137.6 2.6 fusion.14
  140.2 7.8 %convolution_convert_fusion.2 = bf16[384,1024]{1,0:T(8,128)(2,1)S(1)} fusion(bf16[4096,1024]{1,0:T(8,128)(2,1)} %bitcast.1, bf16[384,4096]{1,0:T(8,128)(2,1)} %all-gather.8.cloned.1.call-done, f32[4096]{0:T(1024)S(1)} %convert_element_type.46, f32[384]{0:T(512)S(1)} %add_rsqrt_fusion), kind=kOutput, calls=%fused_computation.47 | convolution fusion | flops 3227910144 | bytes 12338688 | tf_op jit(solution)/shard_map/dot_general | solution.py:67
  148.0 4.7 all-gather.12.cloned.1.call-done
  152.8 7.8 %convolution_convert_fusion = bf16[384,1024]{1,0:T(8,128)(2,1)S(1)} fusion(bf16[4096,1024]{1,0:T(8,128)(2,1)} %all-gather.12.cloned.1.call-done, bf16[384,4096]{1,0:T(8,128)(2,1)} %all-gather.8.cloned.1.call-done, f32[4096]{0:T(1024)S(1)} %convert_element_type.46, f32[384]{0:T(512)S(1)} %add_rsqrt_fusion), kind=kOutput, calls=%fused_computation.45 | convolution fusion | flops 3227910144 | bytes 12338688 | tf_op jit(solution)/shard_map/dot_general | solution.py:67
  160.6 49.1 %all-gather.10.cloned.1.call-done = bf16[4096,1024]{1,0:T(8,128)(2,1)} async-done(((bf16[512,1024]{1,0:T(8,128)(2,1)}), bf16[4096,1024]{1,0:T(8,128)(2,1)}) %all-gather.10.cloned.1.call-update) | async-done | bytes 8388624 | tf_op jit(solution)/shard_map/all_gather | solution.py:70
  209.7 7.8 %convolution_convert_fusion.1 = bf16[384,1024]{1,0:T(8,128)(2,1)S(1)} fusion(bf16[4096,1024]{1,0:T(8,128)(2,1)} %all-gather.10.cloned.1.call-done, bf16[384,4096]{1,0:T(8,128)(2,1)} %all-gather.8.cloned.1.call-done, f32[4096]{0:T(1024)S(1)} %convert_element_type.46, f32[384]{0:T(512)S(1)} %add_rsqrt_fusion), kind=kOutput, calls=%fused_computation.46 | convolution fusion | flops 3227910144 | bytes 12338688 | tf_op jit(solution)/shard_map/dot_general | solution.py:67
  217.5 2.2 collective-permute-start
  219.7 1.2 copy.44
  221.0 18.6 %gather_fusion = f32[4096,1024]{1,0:T(8,128)} fusion(f32[64,1024]{1,0:T(8,128)S(1)} %bitcast.58, s32[4096]{0:T(1024)S(1)} %broadcast_clamp_fusion), kind=kCustom, calls=%fused_computation | custom fusion | bytes 33570816 | tf_op jit(solution)/shard_map/gather | solution.py:94
  239.6 30.9 %copy.31 = f32[64,64,1024]{1,0,2:T(8,128)} copy(f32[64,64,1024]{2,1,0:T(8,128)} %bitcast.59) | data formatting | bytes 33554432 | tf_op jit(solution)/shard_map/gather | solution.py:94
  270.5 2.1 copy.48
  272.6 0.7 maximum_convert_fusion
  273.3 1.4 fusion.17
  274.7 2.2 copy-done.2
  276.9 0.3 slice_multiply_fusion.3
  277.2 2.7 copy.32
  280.0 16.9 %fusion.24 = f32[6,1024,16]{2,0,1:T(8,128)} fusion(f32[6,64,1024]{1,0,2:T(8,128)} %copy.32, f32[64]{0:T(128)S(1)} %broadcast_subtract_fusion, f32[1024,16]{1,0:T(8,128)S(1)} %copy.30), kind=kOutput, calls=%fused_computation.39 | convolution fusion | flops 76546048 | bytes 2031872 | tf_op jit(solution)/shard_map/sck,bsc->bck/dot_general | solution.py:98
  296.8 2.7 copy.34
  299.5 0.4 while.27
  299.9 10.2 %all-gather.1 = f32[8192,16]{0,1:T(8,128)S(1)} all-gather(f32[1024,16]{0,1:T(8,128)S(1)} %get-tuple-element.128), channel_id=3, replica_groups=mesh['ctx'=8,'dp'=4] {'ctx'}, dimensions={0}, use_global_device_ids=true | all-gather | bytes 589824 | tf_op jit(solution)/shard_map/all_gather | solution.py:22
  310.1 0.3 copy.49
  310.4 9.8 %while.28 = (s32[]{:T(128)}, f32[1024,16]{0,1:T(8,128)S(1)}, s32[]{:T(128)}, f32[8,1024,16]{1,0,2:T(8,128)}, f32[8,1024,16]{1,0,2:T(8,128)S(1)}, /*index=5*/s32[]{:T(128)}, s32[]{:T(128)}) while((s32[]{:T(128)}, f32[1024,16]{0,1:T(8,128)S(1)}, s32[]{:T(128)}, f32[8,1024,16]{1,0,2:T(8,128)}, f32[8,1024,16]{1,0,2:T(8,128)S(1)}, ...), condition=%wide.region_4.5_spmd.clone, body=%wide.region_3.4_spmd.clone.sunk | while | flops 65540 | bytes 524397 | solution.py:34
  310.4 1.1 constant_dynamic-slice_fusion.3
  311.6 1.1 constant_dynamic-slice_fusion.3
  312.8 1.1 constant_dynamic-slice_fusion.3
  314.0 1.1 constant_dynamic-slice_fusion.3
  315.2 1.1 constant_dynamic-slice_fusion.3
  316.5 1.1 constant_dynamic-slice_fusion.3
  317.7 1.1 constant_dynamic-slice_fusion.3
  318.9 1.1 constant_dynamic-slice_fusion.3
  320.3 2.7 copy.38
  323.0 56.2 %fusion.3 = f32[1024,6,64]{2,1,0:T(8,128)S(1)} fusion(f32[6,64,1024]{1,0,2:T(8,128)} %copy.32, f32[64,64,1024]{1,0,2:T(8,128)} %copy.31, pred[64,64]{1,0:T(8,128)(4,1)S(1)} %subtract_compare_fusion), kind=kOutput, calls=%fused_computation.10 | convolution fusion | flops 306184192 | bytes 19927040 | tf_op jit(solution)/shard_map/tsc,bsc->btc/dot_general | solution.py:96
  379.2 12.4 %add_bitcast_fusion = f32[6,64,1024]{1,0,2:T(8,128)} fusion(f32[1024,6,64]{2,1,0:T(8,128)S(1)} %fusion.3, f32[6,1024,16]{2,0,1:T(8,128)S(1)} %copy-done.3, f32[1024,16]{1,0:T(8,128)S(1)} %copy-done.7, f32[64]{0:T(128)S(1)} %broadcast_add_fusion, f32[1024,16]{1,0:T(8,128)S(1)} %copy.30), kind=kOutput, calls=%fused_computation.32 | convolution fusion | flops 77987840 | bytes 3670272 | tf_op jit(solution)/shard_map/tck,bck->btc/dot_general | solution.py:119
  391.6 2.7 copy.39
  394.3 3.9 fusion.29
  398.3 63.5 %all-gather.14.cloned.1.call-done = bf16[384,4096]{1,0:T(8,128)(2,1)} async-done(((bf16[384,1024]{1,0:T(8,128)(2,1)}), bf16[384,4096]{1,0:T(8,128)(2,1)}) %all-gather.14.cloned.1.call-update) | async-done | bytes 3145744 | tf_op jit(solution)/shard_map/all_gather | solution.py:122
  461.8 8.7 %add_convert_fusion = bf16[384,1024]{1,0:T(8,128)(2,1)} fusion(bf16[384,1024]{1,0:T(8,128)(2,1)S(1)} %copy-done.5, bf16[384,4096]{1,0:T(8,128)(2,1)} %all-gather.14.cloned.1.call-done, bf16[4096,1024]{1,0:T(8,128)(2,1)} %all-gather.16.cloned.1.call-done), kind=kOutput, calls=%fused_computation.44 | convolution fusion | flops 3222405120 | bytes 13107200 | tf_op jit(solution)/shard_map/dot_general | solution.py:123
  (78 shorter events, 1.4 us)
Async XLA Ops:
  6.5 1.2 copy-start
  6.5 4.9 %copy-start.4 = (bf16[512,1024]{1,0:T(8,128)(2,1)S(1)}, bf16[512,1024]{1,0:T(8,128)(2,1)}, u32[]{:S(2)}) copy-start(bf16[512,1024]{1,0:T(8,128)(2,1)} %param.18) | copy-start | bytes 3145732
  6.5 131.0 %all-gather.8.cloned.1.call-start = ((), (), s32[]{:S(2)}) async-start(), calls=%async_computation.1 | async-start | bytes 3932160 | tf_op jit(solution)/shard_map/all_gather | solution.py:58
  10.0 142.8 %all-gather.12.cloned.1.call-start = ((), (), s32[]{:S(2)}) async-start(), calls=%async_computation.3 | async-start | bytes 9437184 | tf_op jit(solution)/shard_map/all_gather | solution.py:71
  10.7 198.9 %all-gather.10.cloned.1.call-start = ((), (), s32[]{:S(2)}) async-start(), calls=%async_computation.2 | async-start | bytes 9437184 | tf_op jit(solution)/shard_map/all_gather | solution.py:70
  15.8 6.0 %copy-start.9 = (f32[1024,16]{0,1:T(8,128)S(1)}, f32[1024,16]{0,1:T(8,128)}, u32[]{:S(2)}) copy-start(f32[1024,16]{0,1:T(8,128)} %param.22) | copy-start | bytes 196612
  15.8 6.0 %copy-start.10 = (f32[1024,16]{0,1:T(8,128)S(1)}, f32[1024,16]{0,1:T(8,128)}, u32[]{:S(2)}) copy-start(f32[1024,16]{0,1:T(8,128)} %param.23) | copy-start | bytes 196612
  15.8 6.6 %copy-start.11 = (f32[3,3,1024]{2,1,0:T(4,128)S(1)}, f32[3,3,1024]{2,1,0:T(4,128)}, u32[]{:S(2)}) copy-start(f32[3,3,1024]{2,1,0:T(4,128)} %param.21) | copy-start | bytes 110596
  15.8 124.4 %all-to-all-start = ((bf16[8,512,1024]{2,1,0:T(8,128)(2,1)}), bf16[8,512,1024]{2,1,0:T(8,128)(2,1)}, u32[]{:S(2)}, u32[]{:S(2)}) async-start(bf16[8,512,1024]{2,1,0:T(8,128)(2,1)} %tile.2), calls=%async_computation | async-start | bytes 16777216 | tf_op jit(solution)/shard_map/all_to_all | solution.py:11
  21.1 13.8 %copy-start.13 = (bf16[1024]{0:T(1024)(128)(2,1)S(1)}, bf16[1024]{0:T(1024)(128)(2,1)}, u32[]{:S(2)}) copy-start(bf16[1024]{0:T(1024)(128)(2,1)} %param.17) | copy-start | bytes 6148
  21.1 377.1 %all-gather.16.cloned.1.call-start = ((), (), s32[]{:S(2)}) async-start(), calls=%async_computation.5 | async-start | bytes 9437184 | tf_op jit(solution)/shard_map/all_gather | solution.py:125
  21.7 440.1 %all-gather.14.cloned.1.call-start = ((), (), s32[]{:S(2)}) async-start(), calls=%async_computation.4 | async-start | bytes 3932160 | tf_op jit(solution)/shard_map/all_gather | solution.py:122
  22.0 118.2 %copy-start.6 = (f32[1024,16]{1,0:T(8,128)}, f32[1024,16]{1,0:T(8,128)S(1)}, u32[]{:S(2)}) copy-start(f32[1024,16]{1,0:T(8,128)S(1)} %copy.47) | copy-start | bytes 196612
  217.5 55.1 %collective-permute-start = (bf16[2,3072]{1,0:T(2,128)(2,1)S(1)}, bf16[2,3072]{1,0:T(2,128)(2,1)S(1)}, u32[]{:S(2)}, u32[]{:S(2)}) collective-permute-start(bf16[2,3072]{1,0:T(2,128)(2,1)S(1)} %pad_maximum_fusion), channel_id=1, source_target_pairs={{0,4},{4,8},{8,12},{12,16},{16,20},{20,24},{24,28},{1,5},{5,9},{9,... | collective-permute-start | bytes 36872 | tf_op jit(solution)/shard_map/ppermute | solution.py:17
  274.7 2.2 copy-start.2
  280.0 19.5 %copy-start.8 = (f32[6,1024,16]{1,2,0:T(8,128)S(1)}, f32[6,1024,16]{1,2,0:T(8,128)}, u32[]{:S(2)}) copy-start(f32[6,1024,16]{1,2,0:T(8,128)} %custom-call.4) | copy-start | bytes 1179652
  323.0 56.2 %copy-start.3 = (f32[6,1024,16]{2,0,1:T(8,128)S(1)}, f32[6,1024,16]{2,0,1:T(8,128)}, u32[]{:S(2)}) copy-start(f32[6,1024,16]{2,0,1:T(8,128)} %copy.38) | copy-start | bytes 1179652
  323.0 56.2 %copy-start.7 = (f32[1024,16]{1,0:T(8,128)S(1)}, f32[1024,16]{1,0:T(8,128)}, u32[]{:S(2)}) copy-start(f32[1024,16]{1,0:T(8,128)} %copy-done.6) | copy-start | bytes 196612
  391.6 2.7 copy-start.12
  394.3 67.5 %copy-start.5 = (bf16[384,1024]{1,0:T(8,128)(2,1)S(1)}, bf16[384,1024]{1,0:T(8,128)(2,1)}, u32[]{:S(2)}) copy-start(bf16[384,1024]{1,0:T(8,128)(2,1)} %convolution_convert_fusion.3) | copy-start | bytes 2359300
  461.8 8.7 %copy-start.1 = (bf16[512,1024]{1,0:T(8,128)(2,1)S(1)}, bf16[512,1024]{1,0:T(8,128)(2,1)}, u32[]{:S(2)}) copy-start(bf16[512,1024]{1,0:T(8,128)(2,1)} %param.16) | copy-start | bytes 3145732
Sparse Core Ops, SparseCore 0:
  10.1 66.2 all-gather.7
  78.3 74.4 all-gather.11
  154.7 54.9 all-gather.9
  211.4 54.2 all-gather.15
  398.4 63.4 all-gather.13
